TPU v7x, 128 devices: a whole 4x4x4 slice. The times are simulated.
128 devices in a mesh: rows: 16 (over x, z), cols: 8 (over y, core).
Axes of the slice: x: 4, y: 4, z: 4, core: 2. Of those that a mesh axis runs over, the one named last changes fastest.
Arguments:
- panel_cols: bfloat16 [64, 32, 256, 128], P('rows', 'cols'), may hold values from -1.75 to 1.75
- pivot_inv: bfloat16 [32, 256, 256], P('cols'), may hold values from -0.375 to 0.375
- pivot_rows: bfloat16 [32, 48, 256, 128], P('rows', 'cols'), may hold values from -1.75 to 1.75
- target_factors: bfloat16 [64, 48, 256, 128], P('rows', 'cols'), may hold values from -5 to 5
- near_blocks: bfloat16 [64, 8, 256, 256], P('rows', 'cols'), may hold values from -6 to 6
- near_cols: int32 [64, 8], P('rows', 'cols'), may hold values from 0 to 5, as said below
- sketch: bfloat16 [48, 256, 64], P('cols'), may hold values from -6 to 6
Outputs:
- near_out: bfloat16 [64, 8, 256, 256], P('rows', 'cols')
- far_out: bfloat16 [64, 48, 256, 128], P('rows', 'cols')
Inputs may be any that keep to these rules, and one draw needn't show every extreme that they name: `near_cols`: for every block row, the 1 entries of each group of slots s with equal s // 1 are distinct.
All inputs are finite; a program needn't handle non-finite values.
Results may differ from a plain program's by a relative error of at most 0.009.
Values may be sent and summed in bfloat16 or wider, within the bound.
A program may use at most 128 MiB of HBM per device.

v0:
```python
import math
import jax
import jax.numpy as jnp
from jax import lax
from jax.sharding import PartitionSpec as P


def spread(block, axis, holder):
    block = jnp.where(lax.axis_index(axis) == holder, block, jnp.zeros_like(block))
    return lax.psum(block, axis)


def product_of(form, left, right):
    return jnp.einsum(form, left, right, preferred_element_type=jnp.float32)


def row_update(left_row, rows_all, target_row, near_row, near_index, sketch):
    half = left_row.shape[-1] // 2
    root_size = math.sqrt(left_row.shape[1])
    left_x = left_row[..., :half]
    left_y = left_row[..., half:]
    pivot_p = rows_all[..., :half]
    pivot_q = rows_all[..., half:]
    mid_cores = product_of("kbr,kjbs->kjrs", left_y, pivot_p).astype(jnp.bfloat16)
    left_terms = product_of("kbr,kjrs->jkbs", left_x, mid_cores).astype(jnp.bfloat16)
    left_near = jnp.take(left_terms, near_index, axis=0)
    q_near = jnp.take(pivot_q, near_index, axis=1)
    update = product_of("nkbs,kncs->nbc", left_near, q_near)
    near_new = (near_row.astype(jnp.float32) - update).astype(jnp.bfloat16)
    column_ids = jnp.arange(target_row.shape[0], dtype=jnp.int32)
    is_near = jnp.any(near_index[:, None] == column_ids[None, :], axis=0)
    target_u = target_row[..., :half]
    target_v = target_row[..., half:]
    sketch_core = product_of("jbs,jbt->jst", target_v, sketch).astype(jnp.bfloat16)
    pivot_sketch = product_of("kjbs,jbt->jkst", pivot_q, sketch).astype(jnp.bfloat16)
    sampled = product_of("jbs,jst->jbt", target_u, sketch_core) - product_of(
        "jkbs,jkst->jbt", left_terms, pivot_sketch
    )
    gram_matrix = jnp.einsum("jbs,jbt->jst", sampled, sampled, precision=lax.Precision.HIGHEST)
    factor_chol = jnp.linalg.cholesky(gram_matrix)
    orthonormal = lax.linalg.triangular_solve(
        factor_chol, sampled, left_side=False, lower=True, transpose_a=True
    )
    basis = (root_size * orthonormal).astype(jnp.bfloat16)
    basis_core = product_of("jbs,jbt->jst", target_u, basis).astype(jnp.bfloat16)
    left_core = product_of("jkbs,jbt->jkst", left_terms, basis).astype(jnp.bfloat16)
    weights_out = (
        product_of("jbs,jst->jbt", target_v, basis_core)
        - product_of("kjbs,jkst->jbt", pivot_q, left_core)
    ) / root_size
    keep_far = jnp.where(is_near, 0.0, 1.0).astype(jnp.bfloat16)[:, None, None]
    far_new = jnp.concatenate([basis, weights_out.astype(jnp.bfloat16)], axis=-1) * keep_far
    return (near_new, far_new)


def per_device(panel_cols, pivot_inv, pivot_rows, target_factors, near_blocks, near_cols, sketch):
    half = panel_cols.shape[-1] // 2
    col_left = panel_cols[..., :half]
    col_right = panel_cols[..., half:]
    pivot_right = product_of("kab,ikar->ikbr", pivot_inv, col_right).astype(jnp.bfloat16)
    local_panel = jnp.concatenate([col_left, pivot_right], axis=-1)
    panel_all = lax.all_gather(local_panel, "cols", axis=1, tiled=True)
    owned = pivot_rows.shape[0]
    row_count = lax.axis_size("rows")

    def fetch(owner, buffer):
        arrived = spread(pivot_rows, "rows", owner)
        return lax.dynamic_update_slice_in_dim(
            buffer, arrived, (owner * owned).astype(jnp.int32), 0
        )

    empty = jnp.zeros((row_count * owned,) + pivot_rows.shape[1:], jnp.bfloat16)
    rows_all = lax.fori_loop(0, row_count, fetch, empty)

    def one_row(row_items):
        return row_update(row_items[0], rows_all, row_items[1], row_items[2], row_items[3], sketch)

    near_new, far_new = lax.map(one_row, (panel_all, target_factors, near_blocks, near_cols))
    return (near_new, far_new)


def solution(mesh):
    placed = (
        P("rows", "cols", None, None),
        P("cols", None, None),
        P("rows", "cols", None, None),
        P("rows", "cols", None, None),
        P("rows", "cols", None, None),
        P("rows", "cols"),
        P("cols", None, None),
    )
    return jax.shard_map(
        per_device,
        mesh=mesh,
        in_specs=placed,
        out_specs=(P("rows", "cols", None, None), P("rows", "cols", None, None)),
        check_vma=False,
    )
```

profile of v0, /device:TPU:1, one launch (start us, length us, event | category | flops | bytes accessed | tf_op | source)
XLA Modules:
  0.0 2002.7 jit_solution(16693872794983531070)
XLA Ops:
  12.3 7.8 broadcast_in_dim.59
  20.1 1473.8 %while.29 = (s32[]{:T(128)}, bf16[32,6,256,128]{3,2,1,0:T(8,128)(2,1)}, bf16[2,6,256,128]{3,2,1,0:T(8,128)(2,1)S(1)}, s32[]{:T(128)}, u32[]{:T(128)}, /*index=5*/u32[]{:T(128)}, s32[]{:T(128)}, s32[]{:T(128)}, s32[]{:T(128)}) while((s32[]{:T(128)}, bf16[32,6,256,128]{3,2,1,0:T(8,128)(2,1)}, bf16[2,6,256,128]{3,2,1,0:T(8,128)(2,1)S(1)}, ...), condition=%wide.region_2.3_spmd, body=%wide.region_0.2_spmd.sunk | while | flops 786442 | bytes 7864545 | solution.py:73
  21.1 91.7 %all-reduce.2.cloned.1.call-done = bf16[2,6,256,128]{3,2,1,0:T(8,128)(2,1)} async-done(((bf16[2,6,256,128]{3,2,1,0:T(8,128)(2,1)}), bf16[2,6,256,128]{3,2,1,0:T(8,128)(2,1)}) %all-reduce.2.cloned.1.call-update) | async-done | bytes 786448 | tf_op jit(solution)/shard_map/while/body/eval_jaxpr/psum | solution.py:10
  112.8 2.1 constant_dynamic-update-slice_fusion.4
  115.9 89.1 %all-reduce.2.cloned.1.call-done = bf16[2,6,256,128]{3,2,1,0:T(8,128)(2,1)} async-done(((bf16[2,6,256,128]{3,2,1,0:T(8,128)(2,1)}), bf16[2,6,256,128]{3,2,1,0:T(8,128)(2,1)}) %all-reduce.2.cloned.1.call-update) | async-done | bytes 786448 | tf_op jit(solution)/shard_map/while/body/eval_jaxpr/psum | solution.py:10
  207.9 89.1 %all-reduce.2.cloned.1.call-done = bf16[2,6,256,128]{3,2,1,0:T(8,128)(2,1)} async-done(((bf16[2,6,256,128]{3,2,1,0:T(8,128)(2,1)}), bf16[2,6,256,128]{3,2,1,0:T(8,128)(2,1)}) %all-reduce.2.cloned.1.call-update) | async-done | bytes 786448 | tf_op jit(solution)/shard_map/while/body/eval_jaxpr/psum | solution.py:10
  297.0 2.1 constant_dynamic-update-slice_fusion.4
  300.0 88.7 %all-reduce.2.cloned.1.call-done = bf16[2,6,256,128]{3,2,1,0:T(8,128)(2,1)} async-done(((bf16[2,6,256,128]{3,2,1,0:T(8,128)(2,1)}), bf16[2,6,256,128]{3,2,1,0:T(8,128)(2,1)}) %all-reduce.2.cloned.1.call-update) | async-done | bytes 786448 | tf_op jit(solution)/shard_map/while/body/eval_jaxpr/psum | solution.py:10
  391.8 88.7 %all-reduce.2.cloned.1.call-done = bf16[2,6,256,128]{3,2,1,0:T(8,128)(2,1)} async-done(((bf16[2,6,256,128]{3,2,1,0:T(8,128)(2,1)}), bf16[2,6,256,128]{3,2,1,0:T(8,128)(2,1)}) %all-reduce.2.cloned.1.call-update) | async-done | bytes 786448 | tf_op jit(solution)/shard_map/while/body/eval_jaxpr/psum | solution.py:10
  483.6 88.7 %all-reduce.2.cloned.1.call-done = bf16[2,6,256,128]{3,2,1,0:T(8,128)(2,1)} async-done(((bf16[2,6,256,128]{3,2,1,0:T(8,128)(2,1)}), bf16[2,6,256,128]{3,2,1,0:T(8,128)(2,1)}) %all-reduce.2.cloned.1.call-update) | async-done | bytes 786448 | tf_op jit(solution)/shard_map/while/body/eval_jaxpr/psum | solution.py:10
  575.4 89.1 %all-reduce.2.cloned.1.call-done = bf16[2,6,256,128]{3,2,1,0:T(8,128)(2,1)} async-done(((bf16[2,6,256,128]{3,2,1,0:T(8,128)(2,1)}), bf16[2,6,256,128]{3,2,1,0:T(8,128)(2,1)}) %all-reduce.2.cloned.1.call-update) | async-done | bytes 786448 | tf_op jit(solution)/shard_map/while/body/eval_jaxpr/psum | solution.py:10
  667.5 89.1 %all-reduce.2.cloned.1.call-done = bf16[2,6,256,128]{3,2,1,0:T(8,128)(2,1)} async-done(((bf16[2,6,256,128]{3,2,1,0:T(8,128)(2,1)}), bf16[2,6,256,128]{3,2,1,0:T(8,128)(2,1)}) %all-reduce.2.cloned.1.call-update) | async-done | bytes 786448 | tf_op jit(solution)/shard_map/while/body/eval_jaxpr/psum | solution.py:10
  759.6 89.1 %all-reduce.2.cloned.1.call-done = bf16[2,6,256,128]{3,2,1,0:T(8,128)(2,1)} async-done(((bf16[2,6,256,128]{3,2,1,0:T(8,128)(2,1)}), bf16[2,6,256,128]{3,2,1,0:T(8,128)(2,1)}) %all-reduce.2.cloned.1.call-update) | async-done | bytes 786448 | tf_op jit(solution)/shard_map/while/body/eval_jaxpr/psum | solution.py:10
  851.7 88.7 %all-reduce.2.cloned.1.call-done = bf16[2,6,256,128]{3,2,1,0:T(8,128)(2,1)} async-done(((bf16[2,6,256,128]{3,2,1,0:T(8,128)(2,1)}), bf16[2,6,256,128]{3,2,1,0:T(8,128)(2,1)}) %all-reduce.2.cloned.1.call-update) | async-done | bytes 786448 | tf_op jit(solution)/shard_map/while/body/eval_jaxpr/psum | solution.py:10
  943.5 89.1 %all-reduce.2.cloned.1.call-done = bf16[2,6,256,128]{3,2,1,0:T(8,128)(2,1)} async-done(((bf16[2,6,256,128]{3,2,1,0:T(8,128)(2,1)}), bf16[2,6,256,128]{3,2,1,0:T(8,128)(2,1)}) %all-reduce.2.cloned.1.call-update) | async-done | bytes 786448 | tf_op jit(solution)/shard_map/while/body/eval_jaxpr/psum | solution.py:10
  1032.5 2.1 constant_dynamic-update-slice_fusion.4
  1035.6 88.7 %all-reduce.2.cloned.1.call-done = bf16[2,6,256,128]{3,2,1,0:T(8,128)(2,1)} async-done(((bf16[2,6,256,128]{3,2,1,0:T(8,128)(2,1)}), bf16[2,6,256,128]{3,2,1,0:T(8,128)(2,1)}) %all-reduce.2.cloned.1.call-update) | async-done | bytes 786448 | tf_op jit(solution)/shard_map/while/body/eval_jaxpr/psum | solution.py:10
  1127.4 89.1 %all-reduce.2.cloned.1.call-done = bf16[2,6,256,128]{3,2,1,0:T(8,128)(2,1)} async-done(((bf16[2,6,256,128]{3,2,1,0:T(8,128)(2,1)}), bf16[2,6,256,128]{3,2,1,0:T(8,128)(2,1)}) %all-reduce.2.cloned.1.call-update) | async-done | bytes 786448 | tf_op jit(solution)/shard_map/while/body/eval_jaxpr/psum | solution.py:10
  1219.5 88.7 %all-reduce.2.cloned.1.call-done = bf16[2,6,256,128]{3,2,1,0:T(8,128)(2,1)} async-done(((bf16[2,6,256,128]{3,2,1,0:T(8,128)(2,1)}), bf16[2,6,256,128]{3,2,1,0:T(8,128)(2,1)}) %all-reduce.2.cloned.1.call-update) | async-done | bytes 786448 | tf_op jit(solution)/shard_map/while/body/eval_jaxpr/psum | solution.py:10
  1311.3 88.7 %all-reduce.2.cloned.1.call-done = bf16[2,6,256,128]{3,2,1,0:T(8,128)(2,1)} async-done(((bf16[2,6,256,128]{3,2,1,0:T(8,128)(2,1)}), bf16[2,6,256,128]{3,2,1,0:T(8,128)(2,1)}) %all-reduce.2.cloned.1.call-update) | async-done | bytes 786448 | tf_op jit(solution)/shard_map/while/body/eval_jaxpr/psum | solution.py:10
  1403.1 88.7 %all-reduce.2.cloned.1.call-done = bf16[2,6,256,128]{3,2,1,0:T(8,128)(2,1)} async-done(((bf16[2,6,256,128]{3,2,1,0:T(8,128)(2,1)}), bf16[2,6,256,128]{3,2,1,0:T(8,128)(2,1)}) %all-reduce.2.cloned.1.call-update) | async-done | bytes 786448 | tf_op jit(solution)/shard_map/while/body/eval_jaxpr/psum | solution.py:10
  1491.8 2.1 constant_dynamic-update-slice_fusion.4
  1494.5 16.8 copy.60
  1511.4 16.6 copy.62
  1527.9 6.5 fusion.56
  1534.5 4.7 copy.64
  1539.1 7.6 all-gather.2.cloned.1.call-done
  1546.7 447.8 %while.30 = (s32[]{:T(128)}, bf16[4,1,256,256]{3,2,1,0:T(8,128)(2,1)}, bf16[4,6,256,128]{3,2,1,0:T(8,128)(2,1)}, bf16[4,1,256,256]{3,2,1,0:T(8,128)(2,1)}, s32[4...) while((s32[]{:T(128)}, ...), condition=%wide.region_6.7_spmd, body=%wide.region_3.6_spmd.sunk | while | flops 2490991104 | bytes 93083896 | solution.py:78
  1546.7 3.2 constant_dynamic-slice_fusion.6
  1549.9 3.3 copy.105
  1553.2 10.2 convolution_convert_fusion.5
  1563.3 4.9 convolution_bitcast_fusion.3
  1571.4 35.2 %custom-call.15 = f32[6,64,64]{2,1,0:T(8,128)S(1)} custom-call(f32[6,64,64]{2,1,0:T(8,128)S(1)} %fusion.126), custom_call_target="Cholesky" | custom-call | tf_op jit(solution)/shard_map/while/body/eval_jaxpr/jit(cholesky)/cholesky | solution.py:40
  1606.9 29.5 %custom-call.16 = f32[6,1,64,64]{2,3,1,0:T(8,128)S(1)} custom-call(f32[6,1,64,64]{3,2,1,0:T(8,128)S(1)} %select_bitcast_fusion.2), custom_call_target="InvertDiagBlocksLowerTriangular" | custom-call | tf_op jit(solution)/shard_map/while/body/eval_jaxpr/triangular_solve | solution.py:41
  1636.9 7.4 fusion.128
  1648.8 6.3 copy.106
  1656.2 2.5 fusion.124
  1658.7 3.2 constant_dynamic-slice_fusion.6
  1661.9 3.3 copy.105
  1665.1 10.2 convolution_convert_fusion.5
  1675.3 4.9 convolution_bitcast_fusion.3
  1683.4 35.2 %custom-call.15 = f32[6,64,64]{2,1,0:T(8,128)S(1)} custom-call(f32[6,64,64]{2,1,0:T(8,128)S(1)} %fusion.126), custom_call_target="Cholesky" | custom-call | tf_op jit(solution)/shard_map/while/body/eval_jaxpr/jit(cholesky)/cholesky | solution.py:40
  1718.8 29.5 %custom-call.16 = f32[6,1,64,64]{2,3,1,0:T(8,128)S(1)} custom-call(f32[6,1,64,64]{3,2,1,0:T(8,128)S(1)} %select_bitcast_fusion.2), custom_call_target="InvertDiagBlocksLowerTriangular" | custom-call | tf_op jit(solution)/shard_map/while/body/eval_jaxpr/triangular_solve | solution.py:41
  1748.9 7.4 fusion.128
  1760.8 6.3 copy.106
  1768.1 2.5 fusion.124
  1770.7 3.2 constant_dynamic-slice_fusion.6
  1773.8 3.3 copy.105
  1777.1 10.2 convolution_convert_fusion.5
  1787.3 4.9 convolution_bitcast_fusion.3
  1795.3 35.2 %custom-call.15 = f32[6,64,64]{2,1,0:T(8,128)S(1)} custom-call(f32[6,64,64]{2,1,0:T(8,128)S(1)} %fusion.126), custom_call_target="Cholesky" | custom-call | tf_op jit(solution)/shard_map/while/body/eval_jaxpr/jit(cholesky)/cholesky | solution.py:40
  1830.8 29.5 %custom-call.16 = f32[6,1,64,64]{2,3,1,0:T(8,128)S(1)} custom-call(f32[6,1,64,64]{3,2,1,0:T(8,128)S(1)} %select_bitcast_fusion.2), custom_call_target="InvertDiagBlocksLowerTriangular" | custom-call | tf_op jit(solution)/shard_map/while/body/eval_jaxpr/triangular_solve | solution.py:41
  1860.8 7.4 fusion.128
  1872.7 6.3 copy.106
  1880.1 2.5 fusion.124
  1882.6 3.2 constant_dynamic-slice_fusion.6
  1885.8 3.3 copy.105
  1889.1 10.2 convolution_convert_fusion.5
  1899.2 4.9 convolution_bitcast_fusion.3
  1907.3 35.2 %custom-call.15 = f32[6,64,64]{2,1,0:T(8,128)S(1)} custom-call(f32[6,64,64]{2,1,0:T(8,128)S(1)} %fusion.126), custom_call_target="Cholesky" | custom-call | tf_op jit(solution)/shard_map/while/body/eval_jaxpr/jit(cholesky)/cholesky | solution.py:40
  1942.8 29.5 %custom-call.16 = f32[6,1,64,64]{2,3,1,0:T(8,128)S(1)} custom-call(f32[6,1,64,64]{3,2,1,0:T(8,128)S(1)} %select_bitcast_fusion.2), custom_call_target="InvertDiagBlocksLowerTriangular" | custom-call | tf_op jit(solution)/shard_map/while/body/eval_jaxpr/triangular_solve | solution.py:41
  1972.8 7.4 fusion.128
  1984.7 6.3 copy.106
  1992.1 2.5 fusion.124
  (153 shorter events, 77.0 us)
Async XLA Ops:
  8.0 2.4 copy-start
  12.3 7.8 copy-start.2
  20.1 92.7 %all-reduce.2.cloned.1.call-start = ((), (), s32[]{:S(2)}) async-start(), calls=%async_computation.1 | async-start | bytes 1572864 | tf_op jit(solution)/shard_map/while/body/eval_jaxpr/psum | solution.py:10
  114.9 90.0 %all-reduce.2.cloned.1.call-start = ((), (), s32[]{:S(2)}) async-start(), calls=%async_computation.1 | async-start | bytes 1572864 | tf_op jit(solution)/shard_map/while/body/eval_jaxpr/psum | solution.py:10
  207.0 90.0 %all-reduce.2.cloned.1.call-start = ((), (), s32[]{:S(2)}) async-start(), calls=%async_computation.1 | async-start | bytes 1572864 | tf_op jit(solution)/shard_map/while/body/eval_jaxpr/psum | solution.py:10
  299.1 89.7 %all-reduce.2.cloned.1.call-start = ((), (), s32[]{:S(2)}) async-start(), calls=%async_computation.1 | async-start | bytes 1572864 | tf_op jit(solution)/shard_map/while/body/eval_jaxpr/psum | solution.py:10
  390.9 89.7 %all-reduce.2.cloned.1.call-start = ((), (), s32[]{:S(2)}) async-start(), calls=%async_computation.1 | async-start | bytes 1572864 | tf_op jit(solution)/shard_map/while/body/eval_jaxpr/psum | solution.py:10
  482.6 89.7 %all-reduce.2.cloned.1.call-start = ((), (), s32[]{:S(2)}) async-start(), calls=%async_computation.1 | async-start | bytes 1572864 | tf_op jit(solution)/shard_map/while/body/eval_jaxpr/psum | solution.py:10
  574.4 90.0 %all-reduce.2.cloned.1.call-start = ((), (), s32[]{:S(2)}) async-start(), calls=%async_computation.1 | async-start | bytes 1572864 | tf_op jit(solution)/shard_map/while/body/eval_jaxpr/psum | solution.py:10
  666.5 90.0 %all-reduce.2.cloned.1.call-start = ((), (), s32[]{:S(2)}) async-start(), calls=%async_computation.1 | async-start | bytes 1572864 | tf_op jit(solution)/shard_map/while/body/eval_jaxpr/psum | solution.py:10
  758.6 90.0 %all-reduce.2.cloned.1.call-start = ((), (), s32[]{:S(2)}) async-start(), calls=%async_computation.1 | async-start | bytes 1572864 | tf_op jit(solution)/shard_map/while/body/eval_jaxpr/psum | solution.py:10
  850.7 89.7 %all-reduce.2.cloned.1.call-start = ((), (), s32[]{:S(2)}) async-start(), calls=%async_computation.1 | async-start | bytes 1572864 | tf_op jit(solution)/shard_map/while/body/eval_jaxpr/psum | solution.py:10
  942.5 90.0 %all-reduce.2.cloned.1.call-start = ((), (), s32[]{:S(2)}) async-start(), calls=%async_computation.1 | async-start | bytes 1572864 | tf_op jit(solution)/shard_map/while/body/eval_jaxpr/psum | solution.py:10
  1034.6 89.7 %all-reduce.2.cloned.1.call-start = ((), (), s32[]{:S(2)}) async-start(), calls=%async_computation.1 | async-start | bytes 1572864 | tf_op jit(solution)/shard_map/while/body/eval_jaxpr/psum | solution.py:10
  1126.4 90.0 %all-reduce.2.cloned.1.call-start = ((), (), s32[]{:S(2)}) async-start(), calls=%async_computation.1 | async-start | bytes 1572864 | tf_op jit(solution)/shard_map/while/body/eval_jaxpr/psum | solution.py:10
  1218.5 89.7 %all-reduce.2.cloned.1.call-start = ((), (), s32[]{:S(2)}) async-start(), calls=%async_computation.1 | async-start | bytes 1572864 | tf_op jit(solution)/shard_map/while/body/eval_jaxpr/psum | solution.py:10
  1310.3 89.7 %all-reduce.2.cloned.1.call-start = ((), (), s32[]{:S(2)}) async-start(), calls=%async_computation.1 | async-start | bytes 1572864 | tf_op jit(solution)/shard_map/while/body/eval_jaxpr/psum | solution.py:10
  1402.1 89.7 %all-reduce.2.cloned.1.call-start = ((), (), s32[]{:S(2)}) async-start(), calls=%async_computation.1 | async-start | bytes 1572864 | tf_op jit(solution)/shard_map/while/body/eval_jaxpr/psum | solution.py:10
  1493.9 52.8 %all-gather.2.cloned.1.call-start = ((), (), s32[]{:S(2)}) async-start(), calls=%async_computation | async-start | bytes 9437184 | tf_op jit(solution)/shard_map/all_gather | solution.py:62
  1527.9 18.8 copy-start.3
  1994.6 1.0 copy-start.1
Sparse Core Ops, SparseCore 0:
  24.7 87.9 all-reduce.1
  119.5 85.3 all-reduce.1
  211.6 85.3 all-reduce.1
  303.4 85.3 all-reduce.1
  395.2 85.3 all-reduce.1
  487.0 85.3 all-reduce.1
  579.1 85.3 all-reduce.1
  671.2 85.3 all-reduce.1
  763.3 85.3 all-reduce.1
  855.1 85.3 all-reduce.1
  947.2 85.3 all-reduce.1
  1039.0 85.3 all-reduce.1
  1131.1 85.3 all-reduce.1
  1222.9 85.3 all-reduce.1
  1314.7 85.3 all-reduce.1
  1406.5 85.3 all-reduce.1
Sparse Core Ops, SparseCore 1:
  1496.1 50.6 all-gather.1
where the time goes:
time: 2010 us; the launch traced here: 2000 us
  waiting for transfers between devices  1430 us (71%)
  other arithmetic  278 us (14%)
  local copies, waits for them, and re-layouts  151 us (8%)
  matrix products  118 us (6%)
    psum x16, waiting for transfers between devices, spread(): return lax.psum(block, axis)  1430 us
    another operation x16, other arithmetic, row_update(): factor_chol = jnp.linalg.cholesky(gram_matrix)  141 us
    another operation x12, other arithmetic, row_update(): lax.linalg.triangular_solve(factor_chol, sampled, left_side=False, lower=...  118 us
    dot_general x26, matrix products, product_of(): return jnp.einsum(form, left, right, preferred_element_type=jnp.float32)  114 us
  transfers between devices with their start and end apart: 17, of which 17 were waited for; matrix products, arithmetic and copies ran while one was open for 2% of the time, Pallas kernels for 0%

commit v1 on v0

--- a/solution.py
+++ b/solution.py
@@ -7,7 +7,10 @@
 
 def spread(block, axis, holder):
     block = jnp.where(lax.axis_index(axis) == holder, block, jnp.zeros_like(block))
-    return lax.psum(block, axis)
+    state_the_cubes = lambda sample, net_axis: lax.all_gather(sample, axis_name=net_axis).sum(
+        axis=0
+    )
+    return state_the_cubes(block, axis)
 
 
 def product_of(form, left, right):

time: 2010 us -> 2150 us (1.070)
  other arithmetic: 278 us -> 392 us
  waiting for transfers between devices: 1430 us -> 1490 us
    all_gather x0 -> x16, waiting for transfers between devices: none -> 1480 us  [spread(): lax.all_gather(sample, axis_name=net_axis).sum(axis=0)]
    psum x16 -> x0, waiting for transfers between devices: 1430 us -> none  [spread(): return lax.psum(block, axis)]
    reduce_sum x0 -> x16, other arithmetic: none -> 114 us  [spread(): lax.all_gather(sample, axis_name=net_axis).sum(axis=0)]
where the time goes in v1:
time: 2150 us
  waiting for transfers between devices  1490 us (69%)
  other arithmetic  392 us (18%)
  local copies, waits for them, and re-layouts  133 us (6%)
  matrix products  118 us (5%)
    all_gather x16, waiting for transfers between devices, spread(): lax.all_gather(sample, axis_name=net_axis).sum(axis=0)  1480 us
    another operation x16, other arithmetic, row_update(): factor_chol = jnp.linalg.cholesky(gram_matrix)  141 us
    another operation x12, other arithmetic, row_update(): lax.linalg.triangular_solve(factor_chol, sampled, left_side=False, lower=...  118 us
    reduce_sum x16, other arithmetic, spread(): lax.all_gather(sample, axis_name=net_axis).sum(axis=0)  114 us
    dot_general x26, matrix products, product_of(): return jnp.einsum(form, left, right, preferred_element_type=jnp.float32)  114 us
  transfers between devices with their start and end apart: 17, of which 17 were waited for; matrix products, arithmetic and copies ran while one was open for 2% of the time, Pallas kernels for 0%

profile of v1, /device:TPU:1, one launch (start us, length us, event | category | flops | bytes accessed | tf_op | source)
XLA Modules:
  0.0 2152.1 jit_solution(8135223612068258241)
XLA Ops:
  12.3 7.8 broadcast_in_dim.59
  20.1 1624.2 %while.31 = (s32[]{:T(128)}, bf16[32,6,256,128]{3,2,1,0:T(8,128)(2,1)}, bf16[2,6,256,128]{3,2,1,0:T(8,128)(2,1)S(1)}, s32[]{:T(128)}, u32[]{:T(128)}, /*index=5*...) while((s32[]{:T(128)}, bf16[32,6,256,128]{3,2,1,0:T(8,128)(2,1)}, ...), condition=%wide.region_2.3_spmd, body=%wide.region_0.2_spmd.sunk | while | flops 6291466 | bytes 56623336 | solution.py:76
  21.1 96.0 %all-gather.8.cloned.1.call-done = bf16[32,6,256,128]{3,2,1,0:T(8,128)(2,1)} async-done(((bf16[2,6,256,128]{3,2,1,0:T(8,128)(2,1)}), bf16[32,6,256,128]{3,2,1,0:T(8,128)(2,1)}) %all-gather.8.cloned.1.call-update) | async-done | bytes 12582928 | tf_op jit(solution)/shard_map/while/body/eval_jaxpr/all_gather | solution.py:10
  117.1 7.1 reduce_sum.15
  126.2 92.4 %all-gather.8.cloned.1.call-done = bf16[32,6,256,128]{3,2,1,0:T(8,128)(2,1)} async-done(((bf16[2,6,256,128]{3,2,1,0:T(8,128)(2,1)}), bf16[32,6,256,128]{3,2,1,0:T(8,128)(2,1)}) %all-gather.8.cloned.1.call-update) | async-done | bytes 12582928 | tf_op jit(solution)/shard_map/while/body/eval_jaxpr/all_gather | solution.py:10
  218.6 7.1 reduce_sum.15
  227.6 92.4 %all-gather.8.cloned.1.call-done = bf16[32,6,256,128]{3,2,1,0:T(8,128)(2,1)} async-done(((bf16[2,6,256,128]{3,2,1,0:T(8,128)(2,1)}), bf16[32,6,256,128]{3,2,1,0:T(8,128)(2,1)}) %all-gather.8.cloned.1.call-update) | async-done | bytes 12582928 | tf_op jit(solution)/shard_map/while/body/eval_jaxpr/all_gather | solution.py:10
  320.0 7.1 reduce_sum.15
  329.0 92.1 %all-gather.8.cloned.1.call-done = bf16[32,6,256,128]{3,2,1,0:T(8,128)(2,1)} async-done(((bf16[2,6,256,128]{3,2,1,0:T(8,128)(2,1)}), bf16[32,6,256,128]{3,2,1,0:T(8,128)(2,1)}) %all-gather.8.cloned.1.call-update) | async-done | bytes 12582928 | tf_op jit(solution)/shard_map/while/body/eval_jaxpr/all_gather | solution.py:10
  421.1 7.1 reduce_sum.15
  430.2 92.1 %all-gather.8.cloned.1.call-done = bf16[32,6,256,128]{3,2,1,0:T(8,128)(2,1)} async-done(((bf16[2,6,256,128]{3,2,1,0:T(8,128)(2,1)}), bf16[32,6,256,128]{3,2,1,0:T(8,128)(2,1)}) %all-gather.8.cloned.1.call-update) | async-done | bytes 12582928 | tf_op jit(solution)/shard_map/while/body/eval_jaxpr/all_gather | solution.py:10
  522.2 7.1 reduce_sum.15
  531.3 92.1 %all-gather.8.cloned.1.call-done = bf16[32,6,256,128]{3,2,1,0:T(8,128)(2,1)} async-done(((bf16[2,6,256,128]{3,2,1,0:T(8,128)(2,1)}), bf16[32,6,256,128]{3,2,1,0:T(8,128)(2,1)}) %all-gather.8.cloned.1.call-update) | async-done | bytes 12582928 | tf_op jit(solution)/shard_map/while/body/eval_jaxpr/all_gather | solution.py:10
  623.3 7.1 reduce_sum.15
  632.4 92.4 %all-gather.8.cloned.1.call-done = bf16[32,6,256,128]{3,2,1,0:T(8,128)(2,1)} async-done(((bf16[2,6,256,128]{3,2,1,0:T(8,128)(2,1)}), bf16[32,6,256,128]{3,2,1,0:T(8,128)(2,1)}) %all-gather.8.cloned.1.call-update) | async-done | bytes 12582928 | tf_op jit(solution)/shard_map/while/body/eval_jaxpr/all_gather | solution.py:10
  724.8 7.1 reduce_sum.15
  733.9 92.4 %all-gather.8.cloned.1.call-done = bf16[32,6,256,128]{3,2,1,0:T(8,128)(2,1)} async-done(((bf16[2,6,256,128]{3,2,1,0:T(8,128)(2,1)}), bf16[32,6,256,128]{3,2,1,0:T(8,128)(2,1)}) %all-gather.8.cloned.1.call-update) | async-done | bytes 12582928 | tf_op jit(solution)/shard_map/while/body/eval_jaxpr/all_gather | solution.py:10
  826.2 7.1 reduce_sum.15
  835.3 92.4 %all-gather.8.cloned.1.call-done = bf16[32,6,256,128]{3,2,1,0:T(8,128)(2,1)} async-done(((bf16[2,6,256,128]{3,2,1,0:T(8,128)(2,1)}), bf16[32,6,256,128]{3,2,1,0:T(8,128)(2,1)}) %all-gather.8.cloned.1.call-update) | async-done | bytes 12582928 | tf_op jit(solution)/shard_map/while/body/eval_jaxpr/all_gather | solution.py:10
  927.7 7.1 reduce_sum.15
  936.7 92.1 %all-gather.8.cloned.1.call-done = bf16[32,6,256,128]{3,2,1,0:T(8,128)(2,1)} async-done(((bf16[2,6,256,128]{3,2,1,0:T(8,128)(2,1)}), bf16[32,6,256,128]{3,2,1,0:T(8,128)(2,1)}) %all-gather.8.cloned.1.call-update) | async-done | bytes 12582928 | tf_op jit(solution)/shard_map/while/body/eval_jaxpr/all_gather | solution.py:10
  1028.8 7.1 reduce_sum.15
  1037.8 92.4 %all-gather.8.cloned.1.call-done = bf16[32,6,256,128]{3,2,1,0:T(8,128)(2,1)} async-done(((bf16[2,6,256,128]{3,2,1,0:T(8,128)(2,1)}), bf16[32,6,256,128]{3,2,1,0:T(8,128)(2,1)}) %all-gather.8.cloned.1.call-update) | async-done | bytes 12582928 | tf_op jit(solution)/shard_map/while/body/eval_jaxpr/all_gather | solution.py:10
  1130.2 7.1 reduce_sum.15
  1139.3 92.1 %all-gather.8.cloned.1.call-done = bf16[32,6,256,128]{3,2,1,0:T(8,128)(2,1)} async-done(((bf16[2,6,256,128]{3,2,1,0:T(8,128)(2,1)}), bf16[32,6,256,128]{3,2,1,0:T(8,128)(2,1)}) %all-gather.8.cloned.1.call-update) | async-done | bytes 12582928 | tf_op jit(solution)/shard_map/while/body/eval_jaxpr/all_gather | solution.py:10
  1231.4 7.1 reduce_sum.15
  1240.4 92.4 %all-gather.8.cloned.1.call-done = bf16[32,6,256,128]{3,2,1,0:T(8,128)(2,1)} async-done(((bf16[2,6,256,128]{3,2,1,0:T(8,128)(2,1)}), bf16[32,6,256,128]{3,2,1,0:T(8,128)(2,1)}) %all-gather.8.cloned.1.call-update) | async-done | bytes 12582928 | tf_op jit(solution)/shard_map/while/body/eval_jaxpr/all_gather | solution.py:10
  1332.8 7.1 reduce_sum.15
  1341.9 92.1 %all-gather.8.cloned.1.call-done = bf16[32,6,256,128]{3,2,1,0:T(8,128)(2,1)} async-done(((bf16[2,6,256,128]{3,2,1,0:T(8,128)(2,1)}), bf16[32,6,256,128]{3,2,1,0:T(8,128)(2,1)}) %all-gather.8.cloned.1.call-update) | async-done | bytes 12582928 | tf_op jit(solution)/shard_map/while/body/eval_jaxpr/all_gather | solution.py:10
  1433.9 7.1 reduce_sum.15
  1443.0 92.1 %all-gather.8.cloned.1.call-done = bf16[32,6,256,128]{3,2,1,0:T(8,128)(2,1)} async-done(((bf16[2,6,256,128]{3,2,1,0:T(8,128)(2,1)}), bf16[32,6,256,128]{3,2,1,0:T(8,128)(2,1)}) %all-gather.8.cloned.1.call-update) | async-done | bytes 12582928 | tf_op jit(solution)/shard_map/while/body/eval_jaxpr/all_gather | solution.py:10
  1535.1 7.1 reduce_sum.15
  1544.1 92.1 %all-gather.8.cloned.1.call-done = bf16[32,6,256,128]{3,2,1,0:T(8,128)(2,1)} async-done(((bf16[2,6,256,128]{3,2,1,0:T(8,128)(2,1)}), bf16[32,6,256,128]{3,2,1,0:T(8,128)(2,1)}) %all-gather.8.cloned.1.call-update) | async-done | bytes 12582928 | tf_op jit(solution)/shard_map/while/body/eval_jaxpr/all_gather | solution.py:10
  1636.2 7.1 reduce_sum.15
  1644.9 16.8 copy.60
  1661.6 16.6 copy.62
  1678.2 6.4 fusion.56
  1684.6 4.7 copy.64
  1689.3 6.8 all-gather.6.cloned.1.call-done
  1696.1 447.8 %while.32 = (s32[]{:T(128)}, bf16[4,1,256,256]{3,2,1,0:T(8,128)(2,1)}, bf16[4,6,256,128]{3,2,1,0:T(8,128)(2,1)}, bf16[4,1,256,256]{3,2,1,0:T(8,128)(2,1)}, s32[4...) while((s32[]{:T(128)}, ...), condition=%wide.region_6.7_spmd, body=%wide.region_3.6_spmd.sunk | while | flops 2490991104 | bytes 93083896 | solution.py:81
  1702.5 10.2 convolution_convert_fusion.5
  1712.7 4.9 convolution_bitcast_fusion.3
  1720.8 35.2 %custom-call.15 = f32[6,64,64]{2,1,0:T(8,128)S(1)} custom-call(f32[6,64,64]{2,1,0:T(8,128)S(1)} %fusion.126), custom_call_target="Cholesky" | custom-call | tf_op jit(solution)/shard_map/while/body/eval_jaxpr/jit(cholesky)/cholesky | solution.py:43
  1756.2 29.5 %custom-call.16 = f32[6,1,64,64]{2,3,1,0:T(8,128)S(1)} custom-call(f32[6,1,64,64]{3,2,1,0:T(8,128)S(1)} %select_bitcast_fusion.2), custom_call_target="InvertDiagBlocksLowerTriangular" | custom-call | tf_op jit(solution)/shard_map/while/body/eval_jaxpr/triangular_solve | solution.py:44
  1786.3 7.4 fusion.128
  1798.1 6.3 copy.106
  1814.5 10.2 convolution_convert_fusion.5
  1824.6 4.9 convolution_bitcast_fusion.3
  1832.7 35.2 %custom-call.15 = f32[6,64,64]{2,1,0:T(8,128)S(1)} custom-call(f32[6,64,64]{2,1,0:T(8,128)S(1)} %fusion.126), custom_call_target="Cholesky" | custom-call | tf_op jit(solution)/shard_map/while/body/eval_jaxpr/jit(cholesky)/cholesky | solution.py:43
  1868.2 29.5 %custom-call.16 = f32[6,1,64,64]{2,3,1,0:T(8,128)S(1)} custom-call(f32[6,1,64,64]{3,2,1,0:T(8,128)S(1)} %select_bitcast_fusion.2), custom_call_target="InvertDiagBlocksLowerTriangular" | custom-call | tf_op jit(solution)/shard_map/while/body/eval_jaxpr/triangular_solve | solution.py:44
  1898.2 7.4 fusion.128
  1910.1 6.3 copy.106
  1926.4 10.2 convolution_convert_fusion.5
  1936.6 4.9 convolution_bitcast_fusion.3
  1944.7 35.2 %custom-call.15 = f32[6,64,64]{2,1,0:T(8,128)S(1)} custom-call(f32[6,64,64]{2,1,0:T(8,128)S(1)} %fusion.126), custom_call_target="Cholesky" | custom-call | tf_op jit(solution)/shard_map/while/body/eval_jaxpr/jit(cholesky)/cholesky | solution.py:43
  1980.1 29.5 %custom-call.16 = f32[6,1,64,64]{2,3,1,0:T(8,128)S(1)} custom-call(f32[6,1,64,64]{3,2,1,0:T(8,128)S(1)} %select_bitcast_fusion.2), custom_call_target="InvertDiagBlocksLowerTriangular" | custom-call | tf_op jit(solution)/shard_map/while/body/eval_jaxpr/triangular_solve | solution.py:44
  2010.2 7.4 fusion.128
  2022.1 6.3 copy.106
  2038.4 10.2 convolution_convert_fusion.5
  2048.6 4.9 convolution_bitcast_fusion.3
  2056.6 35.2 %custom-call.15 = f32[6,64,64]{2,1,0:T(8,128)S(1)} custom-call(f32[6,64,64]{2,1,0:T(8,128)S(1)} %fusion.126), custom_call_target="Cholesky" | custom-call | tf_op jit(solution)/shard_map/while/body/eval_jaxpr/jit(cholesky)/cholesky | solution.py:43
  2092.1 29.5 %custom-call.16 = f32[6,1,64,64]{2,3,1,0:T(8,128)S(1)} custom-call(f32[6,1,64,64]{3,2,1,0:T(8,128)S(1)} %select_bitcast_fusion.2), custom_call_target="InvertDiagBlocksLowerTriangular" | custom-call | tf_op jit(solution)/shard_map/while/body/eval_jaxpr/triangular_solve | solution.py:44
  2122.1 7.4 fusion.128
  2134.0 6.3 copy.106
  (169 shorter events, 103.1 us)
Async XLA Ops:
  8.0 2.4 copy-start
  12.3 7.8 copy-start.2
  20.1 97.0 %all-gather.8.cloned.1.call-start = ((), (), s32[]{:S(2)}) async-start(), calls=%async_computation.1 | async-start | bytes 13369344 | tf_op jit(solution)/shard_map/while/body/eval_jaxpr/all_gather | solution.py:10
  125.2 93.3 %all-gather.8.cloned.1.call-start = ((), (), s32[]{:S(2)}) async-start(), calls=%async_computation.1 | async-start | bytes 13369344 | tf_op jit(solution)/shard_map/while/body/eval_jaxpr/all_gather | solution.py:10
  226.6 93.3 %all-gather.8.cloned.1.call-start = ((), (), s32[]{:S(2)}) async-start(), calls=%async_computation.1 | async-start | bytes 13369344 | tf_op jit(solution)/shard_map/while/body/eval_jaxpr/all_gather | solution.py:10
  328.1 93.0 %all-gather.8.cloned.1.call-start = ((), (), s32[]{:S(2)}) async-start(), calls=%async_computation.1 | async-start | bytes 13369344 | tf_op jit(solution)/shard_map/while/body/eval_jaxpr/all_gather | solution.py:10
  429.2 93.0 %all-gather.8.cloned.1.call-start = ((), (), s32[]{:S(2)}) async-start(), calls=%async_computation.1 | async-start | bytes 13369344 | tf_op jit(solution)/shard_map/while/body/eval_jaxpr/all_gather | solution.py:10
  530.3 93.0 %all-gather.8.cloned.1.call-start = ((), (), s32[]{:S(2)}) async-start(), calls=%async_computation.1 | async-start | bytes 13369344 | tf_op jit(solution)/shard_map/while/body/eval_jaxpr/all_gather | solution.py:10
  631.4 93.3 %all-gather.8.cloned.1.call-start = ((), (), s32[]{:S(2)}) async-start(), calls=%async_computation.1 | async-start | bytes 13369344 | tf_op jit(solution)/shard_map/while/body/eval_jaxpr/all_gather | solution.py:10
  732.9 93.3 %all-gather.8.cloned.1.call-start = ((), (), s32[]{:S(2)}) async-start(), calls=%async_computation.1 | async-start | bytes 13369344 | tf_op jit(solution)/shard_map/while/body/eval_jaxpr/all_gather | solution.py:10
  834.3 93.3 %all-gather.8.cloned.1.call-start = ((), (), s32[]{:S(2)}) async-start(), calls=%async_computation.1 | async-start | bytes 13369344 | tf_op jit(solution)/shard_map/while/body/eval_jaxpr/all_gather | solution.py:10
  935.7 93.0 %all-gather.8.cloned.1.call-start = ((), (), s32[]{:S(2)}) async-start(), calls=%async_computation.1 | async-start | bytes 13369344 | tf_op jit(solution)/shard_map/while/body/eval_jaxpr/all_gather | solution.py:10
  1036.9 93.3 %all-gather.8.cloned.1.call-start = ((), (), s32[]{:S(2)}) async-start(), calls=%async_computation.1 | async-start | bytes 13369344 | tf_op jit(solution)/shard_map/while/body/eval_jaxpr/all_gather | solution.py:10
  1138.3 93.0 %all-gather.8.cloned.1.call-start = ((), (), s32[]{:S(2)}) async-start(), calls=%async_computation.1 | async-start | bytes 13369344 | tf_op jit(solution)/shard_map/while/body/eval_jaxpr/all_gather | solution.py:10
  1239.4 93.3 %all-gather.8.cloned.1.call-start = ((), (), s32[]{:S(2)}) async-start(), calls=%async_computation.1 | async-start | bytes 13369344 | tf_op jit(solution)/shard_map/while/body/eval_jaxpr/all_gather | solution.py:10
  1340.9 93.0 %all-gather.8.cloned.1.call-start = ((), (), s32[]{:S(2)}) async-start(), calls=%async_computation.1 | async-start | bytes 13369344 | tf_op jit(solution)/shard_map/while/body/eval_jaxpr/all_gather | solution.py:10
  1442.0 93.0 %all-gather.8.cloned.1.call-start = ((), (), s32[]{:S(2)}) async-start(), calls=%async_computation.1 | async-start | bytes 13369344 | tf_op jit(solution)/shard_map/while/body/eval_jaxpr/all_gather | solution.py:10
  1543.1 93.0 %all-gather.8.cloned.1.call-start = ((), (), s32[]{:S(2)}) async-start(), calls=%async_computation.1 | async-start | bytes 13369344 | tf_op jit(solution)/shard_map/while/body/eval_jaxpr/all_gather | solution.py:10
  1644.3 51.8 %all-gather.6.cloned.1.call-start = ((), (), s32[]{:S(2)}) async-start(), calls=%async_computation | async-start | bytes 9437184 | tf_op jit(solution)/shard_map/all_gather | solution.py:65
  1678.2 17.9 copy-start.3
  2143.9 1.0 copy-start.1
Sparse Core Ops, SparseCore 0:
  23.7 93.3 all-gather.7
  128.8 89.7 all-gather.7
  230.2 89.7 all-gather.7
  331.3 89.7 all-gather.7
  432.5 89.7 all-gather.7
  533.6 89.7 all-gather.7
  635.0 89.7 all-gather.7
  736.5 89.7 all-gather.7
  837.9 89.7 all-gather.7
  939.0 89.7 all-gather.7
  1040.5 89.7 all-gather.7
  1141.6 89.7 all-gather.7
  1243.0 89.7 all-gather.7
  1344.2 89.7 all-gather.7
  1445.3 89.7 all-gather.7
  1546.4 89.7 all-gather.7
Sparse Core Ops, SparseCore 1:
  1646.5 49.5 all-gather.5
